TPU v7x, 32 devices: a whole 2x2x4 slice. The times are simulated.
32 devices in a mesh: parts: 2 (over x), context: 8 (over z, core), tensor: 2 (over y).
Axes of the slice: x: 2, y: 2, z: 4, core: 2. Of those that a mesh axis runs over, the one named last changes fastest.
Arguments:
- queries: bfloat16 [4096, 8192], P(('parts', 'context'), 'tensor'), parts along dimension 0, may hold values from -13 to 13
- keys: bfloat16 [4096, 1024], P(('parts', 'context'), 'tensor'), parts along dimension 0, may hold values from -5.2 to 5.2
- values: bfloat16 [4096, 1024], P(('parts', 'context'), 'tensor'), parts along dimension 0, may hold values from -6 to 6
- out_weight: bfloat16 [8192, 4096], P('tensor'), may hold values from -0.1875 to 0.1875
Outputs:
- mixed: bfloat16 [4096, 4096], P(('parts', 'context'), 'tensor'), parts along dimension 0
There are 2 independent parts, one for each index of `parts`. A program takes and returns all parts, laid end to end along the dimension named above; an argument that names none is the same for every part. Nothing has to cross between parts.
All inputs are finite; a program needn't handle non-finite values.
Results may differ from a plain program's by a relative error of at most 0.015.
Values may be sent and summed in bfloat16 or wider, within the bound.
A program may use at most 128 MiB of HBM per device.

v0:
```python
import jax
import jax.numpy as jnp
from jax import lax
from jax.sharding import PartitionSpec as P

HD = 128


def shifted(block, axis, distance):
    devices = range(lax.axis_size(axis))
    route = [(i - distance, i) for i in devices if i - distance in devices]
    return lax.ppermute(block, axis, route)


def absorb(running, query_grouped, kv_block, key_pos, query_pos, valid):
    top_run, sum_run, acc_run = running
    span_len = kv_block.shape[1]
    key_grouped = kv_block[0].reshape(span_len, -1, HD)
    value_grouped = kv_block[1].reshape(span_len, -1, HD)
    scores = jnp.einsum(
        "tkgd,nkd->kgtn", query_grouped, key_grouped, preferred_element_type=jnp.float32
    ) * HD ** (-0.5)
    visible = (key_pos[None, :] <= query_pos[:, None]) & valid
    scores = jnp.where(visible[None, None], scores, -jnp.inf)
    top_new = jnp.maximum(top_run, jnp.max(scores, axis=-1))
    shrink = jnp.exp(top_run - top_new)
    weights = jnp.exp(scores - top_new[..., None])
    sum_new = sum_run * shrink + jnp.sum(weights, axis=-1)
    acc_new = acc_run * shrink[..., None] + jnp.einsum(
        "kgtn,nkd->kgtd",
        weights.astype(jnp.bfloat16),
        value_grouped,
        preferred_element_type=jnp.float32,
    )
    return (top_new, sum_new, acc_new)


def body(queries, keys, values, out_weight):
    tok_rows = queries.shape[0]
    kv_local = keys.shape[1] // HD
    q_local = queries.shape[1] // HD
    group_size = q_local // kv_local
    query_grouped = queries.reshape(tok_rows, kv_local, group_size, HD)
    kv_pair = jnp.stack([keys, values])
    here = lax.axis_index("context")
    local_iota = jnp.arange(tok_rows, dtype=jnp.int32)
    query_pos = here * tok_rows + local_iota
    running = (
        jnp.full((kv_local, group_size, tok_rows), -1e30, jnp.float32),
        jnp.zeros((kv_local, group_size, tok_rows), jnp.float32),
        jnp.zeros((kv_local, group_size, tok_rows, HD), jnp.float32),
    )
    running = absorb(running, query_grouped, kv_pair, query_pos, query_pos, True)

    def cycle_turn(turn_idx, carry):
        carried, kv_block = carry
        kv_block = shifted(kv_block, "context", 1)
        source = here - turn_idx
        key_pos = source * tok_rows + local_iota
        carried = absorb(carried, query_grouped, kv_block, key_pos, query_pos, source >= 0)
        return (carried, kv_block)

    running, _ = lax.fori_loop(1, lax.axis_size("context"), cycle_turn, (running, kv_pair))
    top_run, sum_run, acc_run = running
    attended = (acc_run / sum_run[..., None]).astype(jnp.bfloat16)
    attended = attended.transpose(2, 0, 1, 3).reshape(tok_rows, q_local * HD)
    terms = jnp.dot(attended, out_weight, preferred_element_type=jnp.float32)
    return lax.psum_scatter(terms.astype(jnp.bfloat16), "tensor", scatter_dimension=1, tiled=True)


def solution(mesh):
    return jax.shard_map(
        body,
        mesh=mesh,
        in_specs=(
            P(("parts", "context"), "tensor"),
            P(("parts", "context"), "tensor"),
            P(("parts", "context"), "tensor"),
            P("tensor", None),
        ),
        out_specs=P(("parts", "context"), "tensor"),
        check_vma=False,
    )
```

profile of v0, /device:TPU:24, one launch (start us, length us, event | category | flops | bytes accessed | tf_op | source)
XLA Modules:
  0.0 227.8 jit_solution(6164832710145542891)
XLA Ops:
  10.9 4.1 %copy.12 = bf16[256,4096]{0,1:T(8,128)(2,1)} copy(bf16[256,4096]{1,0:T(8,128)(2,1)} %param.6) | data formatting | bytes 4194304 | tf_op args[0]
  15.0 3.0 %copy.19 = bf16[256,4,8,128]{3,0,2,1:T(8,128)(2,1)S(1)} copy(bf16[256,4,8,128]{0,3,2,1:T(8,128)(2,1)} %bitcast.64) | data formatting | bytes 4194304
  18.0 2.9 %fusion.19 = (f32[4,8,256]{2,1,0:T(8,128)S(1)}, f32[4,256,256,8]{2,1,3,0:T(8,128)S(1)}) fusion(pred[256,256]{0,1:T(8,128)(4,1)S(1)} %broadcast_compare_fusion, bf16[256,4,8,128]{0,3,2,1:T(8,128)(2,1)} %bitcast.65, bf16[256,4,128,1]{2,1,0,3:T(4,128)(2,1)S(1)} %bitcast.67), kind=kOutput, calls=%fused_computation.24 | convolution fusion | flops 543154176 | bytes 10846208 | tf_op jit(solution)/shard_map/tkgd,nkd->kgtn/dot_general | solution.py:20
  23.6 4.5 %broadcast_add_fusion = f32[4,8,256,128]{3,2,1,0:T(8,128)} fusion(f32[4,8,256]{2,1,0:T(8,128)S(1)} %get-tuple-element.214, f32[4,256,256,8]{2,1,3,0:T(8,128)S(1)} %get-tuple-element.217, f32[4,8,256]{2,1,0:T(8,128)S(1)} %broadcast_maximum_fusion, pred[256,256]{0,1:T(8,128)(4,1)S(1)} %broadcast_compare_fusion, bf16[256,4,128,1]{2,1,0,3:T(4,128)(2,1)S(1)} %bitcast.70), kind=kOutput, calls=%fused_computation.32 | convolution fusion | flops 546308096 | bytes 12976128 | tf_op jit(solution)/shard_map/kgtn,nkd->kgtd/dot_general | solution.py:29
  28.1 134.8 %while.20 = (s32[]{:T(128)}, f32[4,8,256]{2,1,0:T(8,128)S(1)}, f32[4,8,256]{2,1,0:T(8,128)S(1)}, f32[4,8,256,128]{3,2,1,0:T(8,128)}, bf16[2,256,512]{1,2,0:T(8,1...) while((s32[]{:T(128)}, f32[4,8,256]{2,1,0:T(8,128)S(1)}, ...), condition=%wide.region_5.6_spmd.clone, body=%wide.region_2.5_spmd.clone.sunk | while | flops 1099055616 | bytes 74715384 | solution.py:63
  28.1 1.9 collective-permute-start
  30.1 8.4 %collective-permute-done = bf16[2,256,512]{1,2,0:T(8,128)(2,1)S(1)} collective-permute-done((bf16[2,256,512]{1,2,0:T(8,128)(2,1)S(1)}, bf16[2,256,512]{1,2,0:T(8,128)(2,1)S(1)}, u32[]{:S(2)}, u32[]{:S(2)}) %collective-permute-start) | collective-permute-done | bytes 524320 | tf_op jit(solution)/shard_map/while/body/eval_jaxpr/ppermute | solution.py:12
  42.0 3.5 %multiply_add_fusion.5 = f32[4,8,256,128]{3,2,1,0:T(8,128)S(1)} fusion(f32[4,8,256,128]{3,2,1,0:T(8,128)S(1)} %copy-done, f32[4,8,256]{2,1,0:T(8,128)S(1)} %get-tuple-element.281, bf16[256,4,128,1]{0,2,3,1:T(8,128)(2,1)S(1)} %bitcast.62, f32[4,256,256,8]{2,1,3,0:T(8,128)S(1)} %get-tuple-element.279, f32[4,8,256]{2,1,0:T(8,128)S(1)} %max.9, ...), kind=kOutput, calls=%fused_computation.8.clone.1 | convolution fusion | flops 547356672 | bytes 17170432 | tf_op jit(solution)/shard_map/while/body/eval_jaxpr/kgtn,nkd->kgtd/dot_general | solution.py:29
  45.5 1.9 copy-done.1
  47.4 1.9 collective-permute-start
  49.4 8.4 %collective-permute-done = bf16[2,256,512]{1,2,0:T(8,128)(2,1)S(1)} collective-permute-done((bf16[2,256,512]{1,2,0:T(8,128)(2,1)S(1)}, bf16[2,256,512]{1,2,0:T(8,128)(2,1)S(1)}, u32[]{:S(2)}, u32[]{:S(2)}) %collective-permute-start) | collective-permute-done | bytes 524320 | tf_op jit(solution)/shard_map/while/body/eval_jaxpr/ppermute | solution.py:12
  61.2 3.5 %multiply_add_fusion.5 = f32[4,8,256,128]{3,2,1,0:T(8,128)S(1)} fusion(f32[4,8,256,128]{3,2,1,0:T(8,128)S(1)} %copy-done, f32[4,8,256]{2,1,0:T(8,128)S(1)} %get-tuple-element.281, bf16[256,4,128,1]{0,2,3,1:T(8,128)(2,1)S(1)} %bitcast.62, f32[4,256,256,8]{2,1,3,0:T(8,128)S(1)} %get-tuple-element.279, f32[4,8,256]{2,1,0:T(8,128)S(1)} %max.9, ...), kind=kOutput, calls=%fused_computation.8.clone.1 | convolution fusion | flops 547356672 | bytes 17170432 | tf_op jit(solution)/shard_map/while/body/eval_jaxpr/kgtn,nkd->kgtd/dot_general | solution.py:29
  64.7 1.9 copy-done.1
  66.6 1.9 collective-permute-start
  68.7 8.4 %collective-permute-done = bf16[2,256,512]{1,2,0:T(8,128)(2,1)S(1)} collective-permute-done((bf16[2,256,512]{1,2,0:T(8,128)(2,1)S(1)}, bf16[2,256,512]{1,2,0:T(8,128)(2,1)S(1)}, u32[]{:S(2)}, u32[]{:S(2)}) %collective-permute-start) | collective-permute-done | bytes 524320 | tf_op jit(solution)/shard_map/while/body/eval_jaxpr/ppermute | solution.py:12
  80.5 3.5 %multiply_add_fusion.5 = f32[4,8,256,128]{3,2,1,0:T(8,128)S(1)} fusion(f32[4,8,256,128]{3,2,1,0:T(8,128)S(1)} %copy-done, f32[4,8,256]{2,1,0:T(8,128)S(1)} %get-tuple-element.281, bf16[256,4,128,1]{0,2,3,1:T(8,128)(2,1)S(1)} %bitcast.62, f32[4,256,256,8]{2,1,3,0:T(8,128)S(1)} %get-tuple-element.279, f32[4,8,256]{2,1,0:T(8,128)S(1)} %max.9, ...), kind=kOutput, calls=%fused_computation.8.clone.1 | convolution fusion | flops 547356672 | bytes 17170432 | tf_op jit(solution)/shard_map/while/body/eval_jaxpr/kgtn,nkd->kgtd/dot_general | solution.py:29
  85.9 1.9 collective-permute-start
  87.9 8.4 %collective-permute-done = bf16[2,256,512]{1,2,0:T(8,128)(2,1)S(1)} collective-permute-done((bf16[2,256,512]{1,2,0:T(8,128)(2,1)S(1)}, bf16[2,256,512]{1,2,0:T(8,128)(2,1)S(1)}, u32[]{:S(2)}, u32[]{:S(2)}) %collective-permute-start) | collective-permute-done | bytes 524320 | tf_op jit(solution)/shard_map/while/body/eval_jaxpr/ppermute | solution.py:12
  99.7 3.5 %multiply_add_fusion.5 = f32[4,8,256,128]{3,2,1,0:T(8,128)S(1)} fusion(f32[4,8,256,128]{3,2,1,0:T(8,128)S(1)} %copy-done, f32[4,8,256]{2,1,0:T(8,128)S(1)} %get-tuple-element.281, bf16[256,4,128,1]{0,2,3,1:T(8,128)(2,1)S(1)} %bitcast.62, f32[4,256,256,8]{2,1,3,0:T(8,128)S(1)} %get-tuple-element.279, f32[4,8,256]{2,1,0:T(8,128)S(1)} %max.9, ...), kind=kOutput, calls=%fused_computation.8.clone.1 | convolution fusion | flops 547356672 | bytes 17170432 | tf_op jit(solution)/shard_map/while/body/eval_jaxpr/kgtn,nkd->kgtd/dot_general | solution.py:29
  105.1 1.9 collective-permute-start
  107.2 8.4 %collective-permute-done = bf16[2,256,512]{1,2,0:T(8,128)(2,1)S(1)} collective-permute-done((bf16[2,256,512]{1,2,0:T(8,128)(2,1)S(1)}, bf16[2,256,512]{1,2,0:T(8,128)(2,1)S(1)}, u32[]{:S(2)}, u32[]{:S(2)}) %collective-permute-start) | collective-permute-done | bytes 524320 | tf_op jit(solution)/shard_map/while/body/eval_jaxpr/ppermute | solution.py:12
  119.0 3.5 %multiply_add_fusion.5 = f32[4,8,256,128]{3,2,1,0:T(8,128)S(1)} fusion(f32[4,8,256,128]{3,2,1,0:T(8,128)S(1)} %copy-done, f32[4,8,256]{2,1,0:T(8,128)S(1)} %get-tuple-element.281, bf16[256,4,128,1]{0,2,3,1:T(8,128)(2,1)S(1)} %bitcast.62, f32[4,256,256,8]{2,1,3,0:T(8,128)S(1)} %get-tuple-element.279, f32[4,8,256]{2,1,0:T(8,128)S(1)} %max.9, ...), kind=kOutput, calls=%fused_computation.8.clone.1 | convolution fusion | flops 547356672 | bytes 17170432 | tf_op jit(solution)/shard_map/while/body/eval_jaxpr/kgtn,nkd->kgtd/dot_general | solution.py:29
  124.4 1.9 collective-permute-start
  126.5 8.4 %collective-permute-done = bf16[2,256,512]{1,2,0:T(8,128)(2,1)S(1)} collective-permute-done((bf16[2,256,512]{1,2,0:T(8,128)(2,1)S(1)}, bf16[2,256,512]{1,2,0:T(8,128)(2,1)S(1)}, u32[]{:S(2)}, u32[]{:S(2)}) %collective-permute-start) | collective-permute-done | bytes 524320 | tf_op jit(solution)/shard_map/while/body/eval_jaxpr/ppermute | solution.py:12
  138.3 3.5 %multiply_add_fusion.5 = f32[4,8,256,128]{3,2,1,0:T(8,128)S(1)} fusion(f32[4,8,256,128]{3,2,1,0:T(8,128)S(1)} %copy-done, f32[4,8,256]{2,1,0:T(8,128)S(1)} %get-tuple-element.281, bf16[256,4,128,1]{0,2,3,1:T(8,128)(2,1)S(1)} %bitcast.62, f32[4,256,256,8]{2,1,3,0:T(8,128)S(1)} %get-tuple-element.279, f32[4,8,256]{2,1,0:T(8,128)S(1)} %max.9, ...), kind=kOutput, calls=%fused_computation.8.clone.1 | convolution fusion | flops 547356672 | bytes 17170432 | tf_op jit(solution)/shard_map/while/body/eval_jaxpr/kgtn,nkd->kgtd/dot_general | solution.py:29
  143.7 1.9 collective-permute-start
  145.7 8.4 %collective-permute-done = bf16[2,256,512]{1,2,0:T(8,128)(2,1)S(1)} collective-permute-done((bf16[2,256,512]{1,2,0:T(8,128)(2,1)S(1)}, bf16[2,256,512]{1,2,0:T(8,128)(2,1)S(1)}, u32[]{:S(2)}, u32[]{:S(2)}) %collective-permute-start) | collective-permute-done | bytes 524320 | tf_op jit(solution)/shard_map/while/body/eval_jaxpr/ppermute | solution.py:12
  157.5 3.5 %multiply_add_fusion.5 = f32[4,8,256,128]{3,2,1,0:T(8,128)S(1)} fusion(f32[4,8,256,128]{3,2,1,0:T(8,128)S(1)} %copy-done, f32[4,8,256]{2,1,0:T(8,128)S(1)} %get-tuple-element.281, bf16[256,4,128,1]{0,2,3,1:T(8,128)(2,1)S(1)} %bitcast.62, f32[4,256,256,8]{2,1,3,0:T(8,128)S(1)} %get-tuple-element.279, f32[4,8,256]{2,1,0:T(8,128)S(1)} %max.9, ...), kind=kOutput, calls=%fused_computation.8.clone.1 | convolution fusion | flops 547356672 | bytes 17170432 | tf_op jit(solution)/shard_map/while/body/eval_jaxpr/kgtn,nkd->kgtd/dot_general | solution.py:29
  162.9 5.4 %copy.20 = f32[4,8,256,128]{2,3,1,0:T(8,128)} copy(f32[4,8,256,128]{3,2,1,0:T(8,128)} %get-tuple-element.160) | data formatting | bytes 8388608 | tf_op jit(solution)/shard_map/while | solution.py:63
  168.3 2.7 %divide_convert_fusion = bf16[4,8,256,128]{2,3,1,0:T(8,128)(2,1)S(1)} fusion(f32[4,8,256,128]{2,3,1,0:T(8,128)} %copy.20, f32[4,8,256]{2,1,0:T(8,128)S(1)} %get-tuple-element.161), kind=kLoop, calls=%fused_computation.27 | loop fusion | flops 2097152 | bytes 6324224 | tf_op jit(solution)/shard_map/convert_element_type | solution.py:65
  171.0 16.9 %convolution_convert_fusion = bf16[256,4096]{1,0:T(8,128)(2,1)} fusion(bf16[256,4096]{0,1:T(8,128)(2,1)S(1)} %bitcast.66, bf16[4096,4096]{1,0:T(8,128)(2,1)} %param.9), kind=kOutput, calls=%fused_computation.25 | convolution fusion | flops 8590983168 | bytes 37748736 | tf_op jit(solution)/shard_map/dot_general | solution.py:67
  187.9 33.0 %reduce-scatter.2.cloned.1.call-done = bf16[256,2048]{1,0:T(8,128)(2,1)} async-done(((bf16[256,4096]{1,0:T(8,128)(2,1)}), bf16[256,2048]{1,0:T(8,128)(2,1)}) %reduce-scatter.2.cloned.1.call-update) | async-done | bytes 1048592 | tf_op jit(solution)/shard_map/reduce_scatter | solution.py:68
  (103 shorter events, 40.7 us)
Async XLA Ops:
  6.5 214.4 %reduce-scatter.2.cloned.1.call-start = ((), (), s32[]{:S(2)}) async-start(), calls=%async_computation.1 | async-start | bytes 3145728 | tf_op jit(solution)/shard_map/reduce_scatter | solution.py:68
  23.6 4.5 %copy-start.2 = (bf16[2,256,512]{1,2,0:T(8,128)(2,1)S(1)}, bf16[2,256,512]{1,2,0:T(8,128)(2,1)}, u32[]{:S(2)}) copy-start(bf16[2,256,512]{1,2,0:T(8,128)(2,1)} %pad_maximum_fusion) | copy-start | bytes 1572868
  28.1 10.5 %collective-permute-start = (bf16[2,256,512]{1,2,0:T(8,128)(2,1)S(1)}, bf16[2,256,512]{1,2,0:T(8,128)(2,1)S(1)}, u32[]{:S(2)}, u32[]{:S(2)}) collective-permute-start(bf16[2,256,512]{1,2,0:T(8,128)(2,1)S(1)} %get-tuple-element.298), channel_id=1, source_target_pairs={{0,2},{2,4},{4,6},{6,8},{8,10},{10,12},{12,14},{1,3},{3,5},{5,7},{... | collective-permute-start | bytes 1572872 | tf_op jit(solution)/shard_map/while/body/eval_jaxpr/ppermute | solution.py:12
  38.6 3.3 %copy-start = (f32[4,8,256,128]{3,2,1,0:T(8,128)S(1)}, f32[4,8,256,128]{3,2,1,0:T(8,128)}, u32[]{:S(2)}) copy-start(f32[4,8,256,128]{3,2,1,0:T(8,128)} %get-tuple-element.297) | copy-start | bytes 12582916 | tf_op jit(solution)/shard_map/while
  45.4 1.9 copy-start.1
  47.4 10.5 %collective-permute-start = (bf16[2,256,512]{1,2,0:T(8,128)(2,1)S(1)}, bf16[2,256,512]{1,2,0:T(8,128)(2,1)S(1)}, u32[]{:S(2)}, u32[]{:S(2)}) collective-permute-start(bf16[2,256,512]{1,2,0:T(8,128)(2,1)S(1)} %get-tuple-element.298), channel_id=1, source_target_pairs={{0,2},{2,4},{4,6},{6,8},{8,10},{10,12},{12,14},{1,3},{3,5},{5,7},{... | collective-permute-start | bytes 1572872 | tf_op jit(solution)/shard_map/while/body/eval_jaxpr/ppermute | solution.py:12
  57.9 3.3 %copy-start = (f32[4,8,256,128]{3,2,1,0:T(8,128)S(1)}, f32[4,8,256,128]{3,2,1,0:T(8,128)}, u32[]{:S(2)}) copy-start(f32[4,8,256,128]{3,2,1,0:T(8,128)} %get-tuple-element.297) | copy-start | bytes 12582916 | tf_op jit(solution)/shard_map/while
  64.7 1.9 copy-start.1
  66.6 10.5 %collective-permute-start = (bf16[2,256,512]{1,2,0:T(8,128)(2,1)S(1)}, bf16[2,256,512]{1,2,0:T(8,128)(2,1)S(1)}, u32[]{:S(2)}, u32[]{:S(2)}) collective-permute-start(bf16[2,256,512]{1,2,0:T(8,128)(2,1)S(1)} %get-tuple-element.298), channel_id=1, source_target_pairs={{0,2},{2,4},{4,6},{6,8},{8,10},{10,12},{12,14},{1,3},{3,5},{5,7},{... | collective-permute-start | bytes 1572872 | tf_op jit(solution)/shard_map/while/body/eval_jaxpr/ppermute | solution.py:12
  77.1 3.3 %copy-start = (f32[4,8,256,128]{3,2,1,0:T(8,128)S(1)}, f32[4,8,256,128]{3,2,1,0:T(8,128)}, u32[]{:S(2)}) copy-start(f32[4,8,256,128]{3,2,1,0:T(8,128)} %get-tuple-element.297) | copy-start | bytes 12582916 | tf_op jit(solution)/shard_map/while
  83.9 1.9 copy-start.1
  85.9 10.5 %collective-permute-start = (bf16[2,256,512]{1,2,0:T(8,128)(2,1)S(1)}, bf16[2,256,512]{1,2,0:T(8,128)(2,1)S(1)}, u32[]{:S(2)}, u32[]{:S(2)}) collective-permute-start(bf16[2,256,512]{1,2,0:T(8,128)(2,1)S(1)} %get-tuple-element.298), channel_id=1, source_target_pairs={{0,2},{2,4},{4,6},{6,8},{8,10},{10,12},{12,14},{1,3},{3,5},{5,7},{... | collective-permute-start | bytes 1572872 | tf_op jit(solution)/shard_map/while/body/eval_jaxpr/ppermute | solution.py:12
  96.4 3.3 %copy-start = (f32[4,8,256,128]{3,2,1,0:T(8,128)S(1)}, f32[4,8,256,128]{3,2,1,0:T(8,128)}, u32[]{:S(2)}) copy-start(f32[4,8,256,128]{3,2,1,0:T(8,128)} %get-tuple-element.297) | copy-start | bytes 12582916 | tf_op jit(solution)/shard_map/while
  103.2 1.9 copy-start.1
  105.1 10.5 %collective-permute-start = (bf16[2,256,512]{1,2,0:T(8,128)(2,1)S(1)}, bf16[2,256,512]{1,2,0:T(8,128)(2,1)S(1)}, u32[]{:S(2)}, u32[]{:S(2)}) collective-permute-start(bf16[2,256,512]{1,2,0:T(8,128)(2,1)S(1)} %get-tuple-element.298), channel_id=1, source_target_pairs={{0,2},{2,4},{4,6},{6,8},{8,10},{10,12},{12,14},{1,3},{3,5},{5,7},{... | collective-permute-start | bytes 1572872 | tf_op jit(solution)/shard_map/while/body/eval_jaxpr/ppermute | solution.py:12
  115.7 3.3 %copy-start = (f32[4,8,256,128]{3,2,1,0:T(8,128)S(1)}, f32[4,8,256,128]{3,2,1,0:T(8,128)}, u32[]{:S(2)}) copy-start(f32[4,8,256,128]{3,2,1,0:T(8,128)} %get-tuple-element.297) | copy-start | bytes 12582916 | tf_op jit(solution)/shard_map/while
  122.5 1.9 copy-start.1
  124.4 10.5 %collective-permute-start = (bf16[2,256,512]{1,2,0:T(8,128)(2,1)S(1)}, bf16[2,256,512]{1,2,0:T(8,128)(2,1)S(1)}, u32[]{:S(2)}, u32[]{:S(2)}) collective-permute-start(bf16[2,256,512]{1,2,0:T(8,128)(2,1)S(1)} %get-tuple-element.298), channel_id=1, source_target_pairs={{0,2},{2,4},{4,6},{6,8},{8,10},{10,12},{12,14},{1,3},{3,5},{5,7},{... | collective-permute-start | bytes 1572872 | tf_op jit(solution)/shard_map/while/body/eval_jaxpr/ppermute | solution.py:12
  134.9 3.3 %copy-start = (f32[4,8,256,128]{3,2,1,0:T(8,128)S(1)}, f32[4,8,256,128]{3,2,1,0:T(8,128)}, u32[]{:S(2)}) copy-start(f32[4,8,256,128]{3,2,1,0:T(8,128)} %get-tuple-element.297) | copy-start | bytes 12582916 | tf_op jit(solution)/shard_map/while
  141.7 1.9 copy-start.1
  143.7 10.5 %collective-permute-start = (bf16[2,256,512]{1,2,0:T(8,128)(2,1)S(1)}, bf16[2,256,512]{1,2,0:T(8,128)(2,1)S(1)}, u32[]{:S(2)}, u32[]{:S(2)}) collective-permute-start(bf16[2,256,512]{1,2,0:T(8,128)(2,1)S(1)} %get-tuple-element.298), channel_id=1, source_target_pairs={{0,2},{2,4},{4,6},{6,8},{8,10},{10,12},{12,14},{1,3},{3,5},{5,7},{... | collective-permute-start | bytes 1572872 | tf_op jit(solution)/shard_map/while/body/eval_jaxpr/ppermute | solution.py:12
  154.2 3.3 %copy-start = (f32[4,8,256,128]{3,2,1,0:T(8,128)S(1)}, f32[4,8,256,128]{3,2,1,0:T(8,128)}, u32[]{:S(2)}) copy-start(f32[4,8,256,128]{3,2,1,0:T(8,128)} %get-tuple-element.297) | copy-start | bytes 12582916 | tf_op jit(solution)/shard_map/while
  161.0 1.9 copy-start.1
Sparse Core Ops, SparseCore 0:
  188.0 32.8 reduce-scatter.1
where the time goes:
time: 230 us; the launch traced here: 228 us
  waiting for transfers between devices  92.1 us (40%)
  matrix products  58.8 us (26%)
  local copies, waits for them, and re-layouts  30.4 us (13%)
  other arithmetic  19 us (8%)
  between operations  13.5 us (6%)
  starting transfers between devices  13.4 us (6%)
    ppermute x7, waiting for transfers between devices, shifted(): return lax.ppermute(block, axis, route)  59 us
    reduce_scatter x1, waiting for transfers between devices, body(): lax.psum_scatter(terms.astype(jnp.bfloat16), 'tensor', scatter_dimension=...  33 us
    dot_general x8, matrix products, absorb(): jnp.einsum('kgtn,nkd->kgtd', weights.astype(jnp.bfloat16), value_grouped,...  28.7 us
    dot_general x1, matrix products, body(): terms = jnp.dot(attended, out_weight, preferred_element_type=jnp.float32)  16.9 us
    reduce_sum x8, other arithmetic, absorb(): sum_new = sum_run * shrink + jnp.sum(weights, axis=-1)  14.3 us
    while x42, local copies, waits for them, and re-layouts  13.4 us
    ppermute x7, starting transfers between devices, shifted(): return lax.ppermute(block, axis, route)  13.4 us
    dot_general x8, matrix products, absorb(): jnp.einsum('tkgd,nkd->kgtn', query_grouped, key_grouped, preferred_elemen...  13.2 us
  transfers between devices with their start and end apart: 8, of which 8 were waited for; matrix products, arithmetic and copies ran while one was open for 0% of the time, Pallas kernels for 0%

commit v1 on v0

v1 whole, which is shorter than its diff:
```python
import functools

import jax
import jax.numpy as jnp
import numpy as np
from jax import lax
from jax.experimental import pallas as pl
from jax.experimental.pallas import tpu as pltpu
from jax.sharding import PartitionSpec as P

HD = 128
F32 = jnp.float32
BF16 = jnp.bfloat16


def kernel(dims, q_hbm, k_hbm, v_hbm, w_hbm, out_ref,
           qs, kvg, wv, acc, top, att, sendbuf, recvbuf,
           q_sem, kv_sem, w_sem, zs_sem, ss_sem, zr_sem, sr_sem, ys_sem, yr_sem):
    C, N, tok, n_kv, group, n_out, width, n_chunk, rows = dims
    c = lax.axis_index("context")
    t = lax.axis_index("tensor")
    z = c // 2
    odd = c % 2
    sibling = c + 1 - 2 * odd
    has_up = c + 2 < C
    has_down = c >= 2
    factor = float(HD ** -0.5 * np.log2(np.e))
    tiles = group * tok // rows

    def block(kv, b):
        return kvg.at[kv, pl.ds(pl.multiple_of(b * tok, tok), tok), :]

    own = [pltpu.make_async_copy(k_hbm, block(0, c), kv_sem.at[0]),
           pltpu.make_async_copy(v_hbm, block(1, c), kv_sem.at[1])]
    for copy in own:
        copy.start()

    def q_copy(h):
        return pltpu.make_async_copy(
            q_hbm.at[:, pl.ds(pl.multiple_of(h * HD, HD), HD)],
            qs.at[h // group, pl.ds(pl.multiple_of((h % group) * tok, tok), tok), :],
            q_sem.at[h])

    @pl.loop(0, n_kv * group)
    def _(h):
        q_copy(h).start()

    barrier = pltpu.get_barrier_semaphore()
    pl.semaphore_signal(barrier, inc=1, device_id={"context": sibling})

    @pl.when(has_up)
    def _():
        pl.semaphore_signal(barrier, inc=1, device_id={"context": c + 2})

    @pl.when(has_down)
    def _():
        pl.semaphore_signal(barrier, inc=1, device_id={"context": c - 2})

    for d in range(1, N):
        pl.semaphore_signal(barrier, inc=1, device_id={"tensor": lax.rem(t + d, N)})
    pl.semaphore_wait(barrier, N + has_up.astype(jnp.int32) + has_down.astype(jnp.int32))

    def up_copy(kv, b):
        return pltpu.make_async_remote_copy(
            src_ref=block(kv, b), dst_ref=block(kv, b),
            send_sem=zs_sem.at[kv, b], recv_sem=zr_sem.at[kv, b],
            device_id={"context": c + 2})

    def side_copy(kv, b):
        return pltpu.make_async_remote_copy(
            src_ref=block(kv, b), dst_ref=block(kv, b),
            send_sem=ss_sem.at[kv, b], recv_sem=sr_sem.at[kv, b],
            device_id={"context": sibling})

    for kv in range(2):
        own[kv].wait()

        @pl.when(has_up)
        def _():
            up_copy(kv, c).start()

        @pl.when(odd == 0)
        def _():
            side_copy(kv, c).start()

    def w_copy(i):
        cols = pl.ds(pl.multiple_of(i * width, width), width)
        return pltpu.make_async_copy(w_hbm.at[:, cols], wv.at[:, cols], w_sem.at[i])

    @pl.loop(0, N * n_chunk)
    def _(i):
        w_copy(i).start()

    @pl.loop(0, n_kv * group)
    def _(h):
        q_copy(h).wait()

    def attend(row0, n_keys, first):
        row0 = pl.multiple_of(row0, tok)

        @pl.loop(0, n_kv * tiles)
        def _(i):
            head = i // tiles
            here = pl.ds(pl.multiple_of((i % tiles) * rows, rows), rows)
            lanes = pl.ds(pl.multiple_of(head * HD, HD), HD)
            key = kvg[0, pl.ds(row0, n_keys), lanes]
            val = kvg[1, pl.ds(row0, n_keys), lanes]
            s = lax.dot_general(qs[head, here, :], key, (((1,), (1,)), ((), ())),
                                preferred_element_type=F32)
            if first:
                r = lax.broadcasted_iota(jnp.int32, s.shape, 0) % tok
                k = lax.broadcasted_iota(jnp.int32, s.shape, 1)
                s = jnp.where(k <= r, s, -1e30)
            parts = [s[:, j * HD:(j + 1) * HD] for j in range(n_keys // HD)]
            m = functools.reduce(jnp.maximum, parts)
            m = jnp.broadcast_to(jnp.max(m, axis=1, keepdims=True), m.shape)
            if not first:
                before = top[head, here, :]
                m = jnp.maximum(before, m)
                shrink = jnp.exp2((before - m) * factor)
            top[head, here, :] = m
            mf = m * factor
            p = jnp.concatenate([jnp.exp2(x * factor - mf).astype(BF16) for x in parts], axis=1)
            both = jnp.concatenate([val, jnp.ones_like(val)], axis=1)
            pv = jnp.dot(p, both, preferred_element_type=F32)
            if not first:
                pv = acc[head, here, :] * jnp.concatenate([shrink, shrink], axis=1) + pv
            acc[head, here, :] = pv

    attend(c * tok, tok, True)

    @pl.when(odd == 1)
    def _():
        for kv in range(2):
            side_copy(kv, sibling).wait_recv()
        attend(sibling * tok, tok, False)

    @pl.loop(1, z + 1)
    def _(i):
        b = c - 2 * i
        for kv in range(2):
            up_copy(kv, b).wait_recv()

            @pl.when(has_up)
            def _():
                up_copy(kv, b).start()

            side_copy(kv, b).start()
        for kv in range(2):
            side_copy(kv, sibling - 2 * i).wait_recv()
        attend((z - i) * 2 * tok, 2 * tok, False)

    @pl.loop(0, n_kv * group)
    def _(h):
        here = pl.ds(pl.multiple_of((h % group) * tok, tok), tok)
        a = acc[h // group, here, :]
        att[:, pl.ds(pl.multiple_of(h * HD, HD), HD)] = (a[:, :HD] / a[:, HD:]).astype(BF16)

    def y_copy(i):
        d = i // n_chunk + 1
        return pltpu.make_async_remote_copy(
            src_ref=sendbuf.at[i], dst_ref=recvbuf.at[i],
            send_sem=ys_sem.at[i], recv_sem=yr_sem.at[i],
            device_id={"tensor": lax.rem(t + d, N)})

    def project(chunk):
        w_copy(chunk).wait()
        cols = pl.ds(pl.multiple_of(chunk * width, width), width)
        return jnp.dot(att[...], wv[:, cols], preferred_element_type=F32).astype(BF16)

    @pl.loop(0, (N - 1) * n_chunk)
    def _(i):
        peer = lax.rem(t + i // n_chunk + 1, N)
        sendbuf[i] = project(peer * n_chunk + i % n_chunk)
        y_copy(i).start()

    @pl.loop(0, n_chunk)
    def _(j):
        total = project(t * n_chunk + j).astype(F32)
        for d in range(N - 1):
            y_copy(d * n_chunk + j).wait_recv()
            total = total + recvbuf[d * n_chunk + j].astype(F32)
        out_ref[:, pl.ds(pl.multiple_of(j * width, width), width)] = total.astype(BF16)

    @pl.loop(0, (N - 1) * n_chunk)
    def _(i):
        y_copy(i).wait_send()

    @pl.when(has_up)
    def _():
        @pl.loop(0, z + 1)
        def _(i):
            for kv in range(2):
                up_copy(kv, c - 2 * i).wait_send()

    @pl.loop(1 - (odd == 0).astype(jnp.int32), z + 1)
    def _(i):
        for kv in range(2):
            side_copy(kv, c - 2 * i).wait_send()


def body(C, N, queries, keys, values, out_weight):
    tok, q_width = queries.shape
    kv_width = keys.shape[1]
    n_kv = kv_width // HD
    group = q_width // kv_width
    n_feat, n_out = out_weight.shape
    own_width = n_out // N
    width = min(512, own_width)
    n_chunk = own_width // width
    rows = 2 * tok
    dims = (C, N, tok, n_kv, group, n_out, width, n_chunk, rows)
    n_send = (N - 1) * n_chunk
    dma = pltpu.SemaphoreType.DMA
    return pl.pallas_call(
        functools.partial(kernel, dims),
        out_shape=jax.ShapeDtypeStruct((tok, own_width), BF16),
        in_specs=[pl.BlockSpec(memory_space=pl.ANY)] * 4,
        out_specs=pl.BlockSpec(memory_space=pltpu.VMEM),
        scratch_shapes=[
            pltpu.VMEM((n_kv, group * tok, HD), BF16),
            pltpu.VMEM((2, C * tok, kv_width), BF16),
            pltpu.VMEM((n_feat, n_out), BF16),
            pltpu.VMEM((n_kv, group * tok, 2 * HD), F32),
            pltpu.VMEM((n_kv, group * tok, HD), F32),
            pltpu.VMEM((tok, q_width), BF16),
            pltpu.VMEM((n_send, tok, width), BF16),
            pltpu.VMEM((n_send, tok, width), BF16),
            dma((n_kv * group,)),
            dma((2,)),
            dma((N * n_chunk,)),
            dma((2, C)),
            dma((2, C)),
            dma((2, C)),
            dma((2, C)),
            dma((n_send,)),
            dma((n_send,)),
        ],
        compiler_params=pltpu.CompilerParams(
            collective_id=0, has_side_effects=True, vmem_limit_bytes=67043328
        ),
    )(queries, keys, values, out_weight)


def solution(mesh):
    C, N = mesh.shape["context"], mesh.shape["tensor"]
    return jax.shard_map(
        functools.partial(body, C, N),
        mesh=mesh,
        in_specs=(
            P(("parts", "context"), "tensor"),
            P(("parts", "context"), "tensor"),
            P(("parts", "context"), "tensor"),
            P("tensor", None),
        ),
        out_specs=P(("parts", "context"), "tensor"),
        check_vma=False,
    )
```

time: 230 us -> 91.7 us (0.40)
  waiting for transfers between devices: 92.1 us -> 0 us
  Pallas kernels: 0 us -> 89.2 us
  matrix products: 58.8 us -> 0 us
  local copies, waits for them, and re-layouts: 30.4 us -> 2.3 us
  other arithmetic: 19 us -> 0 us
  between operations: 13.5 us -> 0.01 us
  starting transfers between devices: 13.4 us -> 0 us
    pallas_call x0 -> x1, Pallas kernels: none -> 89.2 us  [body(): pl.pallas_call(functools.partial(kernel, dims), out_shape=jax.ShapeDtypeS...]
    ppermute x7 -> x0, waiting for transfers between devices: 59 us -> none  [shifted(): return lax.ppermute(block, axis, route)]
    dot_general x17 -> x0, matrix products: 58.8 us -> none  [the longest x8 28.7 us: absorb(): jnp.einsum('kgtn,nkd->kgtd', weights.astype(jnp.bfloat16), value_grouped,...]
    reduce_scatter x1 -> x0, waiting for transfers between devices: 33 us -> none  [body(): lax.psum_scatter(terms.astype(jnp.bfloat16), 'tensor', scatter_dimension=...]
    while x43 -> x0, local copies, waits for them, and re-layouts: 18.8 us -> none
    reduce_sum x8 -> x0, other arithmetic: 14.3 us -> none  [absorb(): sum_new = sum_run * shrink + jnp.sum(weights, axis=-1)]
    ppermute x7 -> x0, starting transfers between devices: 13.4 us -> none  [shifted(): return lax.ppermute(block, axis, route)]
    unnamed x6 -> x1, local copies, waits for them, and re-layouts: 9.31 us -> 2.3 us
  transfers between devices with their start and end apart: 8 -> 0, of which waited for: 8 -> 0; matrix products, arithmetic and copies ran while one was open for 0% -> 0% of each run, Pallas kernels for 0% -> 0%
where the time goes in v1:
time: 91.7 us; the launch traced here: 91.5 us
  Pallas kernels  89.2 us (97%)
  local copies, waits for them, and re-layouts  2.3 us (3%)
    pallas_call x1, Pallas kernels, body(): pl.pallas_call(functools.partial(kernel, dims), out_shape=jax.ShapeDtypeS...  89.2 us
    unnamed x1, local copies, waits for them, and re-layouts  2.3 us

profile of v1, /device:TPU:24, one launch (start us, length us, event | category | flops | bytes accessed | tf_op | source)
XLA Modules:
  0.0 91.5 jit_solution(11507957823540974549)
XLA Ops:
  0.0 89.2 %shard_map.46 = bf16[256,2048]{1,0:T(8,128)(2,1)} custom-call(bf16[256,4096]{1,0:T(8,128)(2,1)} %q_hbm.1, bf16[256,512]{1,0:T(8,128)(2,1)} %k_hbm.1, bf16[256,512]{1,0:T(8,128)(2,1)} %v_hbm.1, bf16[4096,4096]{1,0:T(8,128)(2,1)} %w_hbm.1), custom_call_target="tpu_custom_call" | custom-call | tf_op jit(solution)/shard_map/pallas_call | solution.py:215
  89.2 2.3 %copy.6 = bf16[256,2048]{1,0:T(8,128)(2,1)} copy(bf16[256,2048]{1,0:T(8,128)(2,1)} %shard_map.46) | data formatting | bytes 2097152

commit v2 on v1

--- a/solution.py
+++ b/solution.py
@@ -16,7 +16,7 @@
 def kernel(dims, q_hbm, k_hbm, v_hbm, w_hbm, out_ref,
            qs, kvg, wv, acc, top, att, sendbuf, recvbuf,
            q_sem, kv_sem, w_sem, zs_sem, ss_sem, zr_sem, sr_sem, ys_sem, yr_sem):
-    C, N, tok, n_kv, group, n_out, width, n_chunk, rows = dims
+    C, N, tok, n_kv, group, n_out, width, n_chunk = dims
     c = lax.axis_index("context")
     t = lax.axis_index("tensor")
     z = c // 2
@@ -25,15 +25,14 @@
     has_up = c + 2 < C
     has_down = c >= 2
     factor = float(HD ** -0.5 * np.log2(np.e))
-    tiles = group * tok // rows
-
-    def block(kv, b):
-        return kvg.at[kv, pl.ds(pl.multiple_of(b * tok, tok), tok), :]
-
-    own = [pltpu.make_async_copy(k_hbm, block(0, c), kv_sem.at[0]),
-           pltpu.make_async_copy(v_hbm, block(1, c), kv_sem.at[1])]
-    for copy in own:
-        copy.start()
+
+    def own_copy(kv, head):
+        return pltpu.make_async_copy(
+            (k_hbm, v_hbm)[kv].at[:, pl.ds(head * HD, HD)], kvg.at[head, c, kv], kv_sem.at[kv, head])
+
+    for head in range(n_kv):
+        own_copy(0, head).start()
+        own_copy(1, head).start()
 
     def q_copy(h):
         return pltpu.make_async_copy(
@@ -60,28 +59,29 @@
         pl.semaphore_signal(barrier, inc=1, device_id={"tensor": lax.rem(t + d, N)})
     pl.semaphore_wait(barrier, N + has_up.astype(jnp.int32) + has_down.astype(jnp.int32))
 
-    def up_copy(kv, b):
+    def up_copy(head, b):
         return pltpu.make_async_remote_copy(
-            src_ref=block(kv, b), dst_ref=block(kv, b),
-            send_sem=zs_sem.at[kv, b], recv_sem=zr_sem.at[kv, b],
+            src_ref=kvg.at[head, b], dst_ref=kvg.at[head, b],
+            send_sem=zs_sem.at[head, b], recv_sem=zr_sem.at[head, b],
             device_id={"context": c + 2})
 
-    def side_copy(kv, b):
+    def side_copy(head, b):
         return pltpu.make_async_remote_copy(
-            src_ref=block(kv, b), dst_ref=block(kv, b),
-            send_sem=ss_sem.at[kv, b], recv_sem=sr_sem.at[kv, b],
+            src_ref=kvg.at[head, b], dst_ref=kvg.at[head, b],
+            send_sem=ss_sem.at[head, b], recv_sem=sr_sem.at[head, b],
             device_id={"context": sibling})
 
-    for kv in range(2):
-        own[kv].wait()
+    for head in range(n_kv):
+        own_copy(0, head).wait()
+        own_copy(1, head).wait()
 
         @pl.when(has_up)
         def _():
-            up_copy(kv, c).start()
+            up_copy(head, c).start()
 
         @pl.when(odd == 0)
         def _():
-            side_copy(kv, c).start()
+            side_copy(head, c).start()
 
     def w_copy(i):
         cols = pl.ds(pl.multiple_of(i * width, width), width)
@@ -95,20 +95,22 @@
     def _(h):
         q_copy(h).wait()
 
-    def attend(row0, n_keys, first):
-        row0 = pl.multiple_of(row0, tok)
-
-        @pl.loop(0, n_kv * tiles)
-        def _(i):
-            head = i // tiles
-            here = pl.ds(pl.multiple_of((i % tiles) * rows, rows), rows)
-            lanes = pl.ds(pl.multiple_of(head * HD, HD), HD)
-            key = kvg[0, pl.ds(row0, n_keys), lanes]
-            val = kvg[1, pl.ds(row0, n_keys), lanes]
-            s = lax.dot_general(qs[head, here, :], key, (((1,), (1,)), ((), ())),
-                                preferred_element_type=F32)
+    def attend(head, b0, n_blocks, first):
+        n_keys = n_blocks * tok
+        key = kvg[head, pl.ds(b0, n_blocks), 0].reshape(n_keys, HD)
+        val = kvg[head, pl.ds(b0, n_blocks), 1].reshape(n_keys, HD)
+        both = jnp.concatenate([val, jnp.ones_like(val)], axis=1)
+
+        def scores(g):
+            return lax.dot_general(qs[head, g * tok:(g + 1) * tok, :], key,
+                                   (((1,), (1,)), ((), ())), preferred_element_type=F32)
+
+        s = scores(0)
+        for g in range(group):
+            ahead = scores(g + 1) if g + 1 < group else None
+            here = slice(g * tok, (g + 1) * tok)
             if first:
-                r = lax.broadcasted_iota(jnp.int32, s.shape, 0) % tok
+                r = lax.broadcasted_iota(jnp.int32, s.shape, 0)
                 k = lax.broadcasted_iota(jnp.int32, s.shape, 1)
                 s = jnp.where(k <= r, s, -1e30)
             parts = [s[:, j * HD:(j + 1) * HD] for j in range(n_keys // HD)]
@@ -121,40 +123,44 @@
             top[head, here, :] = m
             mf = m * factor
             p = jnp.concatenate([jnp.exp2(x * factor - mf).astype(BF16) for x in parts], axis=1)
-            both = jnp.concatenate([val, jnp.ones_like(val)], axis=1)
             pv = jnp.dot(p, both, preferred_element_type=F32)
             if not first:
                 pv = acc[head, here, :] * jnp.concatenate([shrink, shrink], axis=1) + pv
             acc[head, here, :] = pv
-
-    attend(c * tok, tok, True)
+            s = ahead
+
+    @pl.loop(0, n_kv)
+    def _(head):
+        attend(head, c, 1, True)
 
     @pl.when(odd == 1)
     def _():
-        for kv in range(2):
-            side_copy(kv, sibling).wait_recv()
-        attend(sibling * tok, tok, False)
-
-    @pl.loop(1, z + 1)
-    def _(i):
+        @pl.loop(0, n_kv)
+        def _(head):
+            side_copy(head, sibling).wait_recv()
+            attend(head, sibling, 1, False)
+
+    @pl.loop(0, z * n_kv)
+    def _(step):
+        i = step // n_kv + 1
+        head = step % n_kv
         b = c - 2 * i
-        for kv in range(2):
-            up_copy(kv, b).wait_recv()
-
-            @pl.when(has_up)
-            def _():
-                up_copy(kv, b).start()
-
-            side_copy(kv, b).start()
-        for kv in range(2):
-            side_copy(kv, sibling - 2 * i).wait_recv()
-        attend((z - i) * 2 * tok, 2 * tok, False)
-
-    @pl.loop(0, n_kv * group)
-    def _(h):
-        here = pl.ds(pl.multiple_of((h % group) * tok, tok), tok)
-        a = acc[h // group, here, :]
-        att[:, pl.ds(pl.multiple_of(h * HD, HD), HD)] = (a[:, :HD] / a[:, HD:]).astype(BF16)
+        up_copy(head, b).wait_recv()
+
+        @pl.when(has_up)
+        def _():
+            up_copy(head, b).start()
+
+        side_copy(head, b).start()
+        side_copy(head, sibling - 2 * i).wait_recv()
+        attend(head, 2 * (z - i), 2, False)
+
+    @pl.loop(0, n_kv)
+    def _(head):
+        for g in range(group):
+            a = acc[head, g * tok:(g + 1) * tok, :]
+            lanes = pl.ds(pl.multiple_of((head * group + g) * HD, HD), HD)
+            att[:, lanes] = (a[:, :HD] / a[:, HD:]).astype(BF16)
 
     def y_copy(i):
         d = i // n_chunk + 1
@@ -190,13 +196,13 @@
     def _():
         @pl.loop(0, z + 1)
         def _(i):
-            for kv in range(2):
-                up_copy(kv, c - 2 * i).wait_send()
+            for head in range(n_kv):
+                up_copy(head, c - 2 * i).wait_send()
 
     @pl.loop(1 - (odd == 0).astype(jnp.int32), z + 1)
     def _(i):
-        for kv in range(2):
-            side_copy(kv, c - 2 * i).wait_send()
+        for head in range(n_kv):
+            side_copy(head, c - 2 * i).wait_send()
 
 
 def body(C, N, queries, keys, values, out_weight):
@@ -206,10 +212,9 @@
     group = q_width // kv_width
     n_feat, n_out = out_weight.shape
     own_width = n_out // N
-    width = min(512, own_width)
+    width = min(256, own_width)
     n_chunk = own_width // width
-    rows = 2 * tok
-    dims = (C, N, tok, n_kv, group, n_out, width, n_chunk, rows)
+    dims = (C, N, tok, n_kv, group, n_out, width, n_chunk)
     n_send = (N - 1) * n_chunk
     dma = pltpu.SemaphoreType.DMA
     return pl.pallas_call(
@@ -219,7 +224,7 @@
         out_specs=pl.BlockSpec(memory_space=pltpu.VMEM),
         scratch_shapes=[
             pltpu.VMEM((n_kv, group * tok, HD), BF16),
-            pltpu.VMEM((2, C * tok, kv_width), BF16),
+            pltpu.VMEM((n_kv, C, 2, tok, HD), BF16),
             pltpu.VMEM((n_feat, n_out), BF16),
             pltpu.VMEM((n_kv, group * tok, 2 * HD), F32),
             pltpu.VMEM((n_kv, group * tok, HD), F32),
@@ -227,12 +232,12 @@
             pltpu.VMEM((n_send, tok, width), BF16),
             pltpu.VMEM((n_send, tok, width), BF16),
             dma((n_kv * group,)),
-            dma((2,)),
+            dma((2, n_kv)),
             dma((N * n_chunk,)),
-            dma((2, C)),
-            dma((2, C)),
-            dma((2, C)),
-            dma((2, C)),
+            dma((n_kv, C)),
+            dma((n_kv, C)),
+            dma((n_kv, C)),
+            dma((n_kv, C)),
             dma((n_send,)),
             dma((n_send,)),
         ],

time: 91.7 us -> 74.9 us (0.82)
  Pallas kernels: 89.2 us -> 71.8 us
    pallas_call x1, Pallas kernels: 89.2 us -> 71.8 us  [body(): pl.pallas_call(functools.partial(kernel, dims), out_shape=jax.ShapeDtypeS...]
where the time goes in v2:
time: 74.9 us; the launch traced here: 74.1 us
  Pallas kernels  71.8 us (96%)
  local copies, waits for them, and re-layouts  2.3 us (3%)
    pallas_call x1, Pallas kernels, body(): pl.pallas_call(functools.partial(kernel, dims), out_shape=jax.ShapeDtypeS...  71.8 us
    unnamed x1, local copies, waits for them, and re-layouts  2.3 us

profile of v2, /device:TPU:24, one launch (start us, length us, event | category | flops | bytes accessed | tf_op | source)
XLA Modules:
  0.0 74.1 jit_solution(3531916788901642193)
XLA Ops:
  0.0 71.8 %shard_map.46 = bf16[256,2048]{1,0:T(8,128)(2,1)} custom-call(bf16[256,4096]{1,0:T(8,128)(2,1)} %q_hbm.1, bf16[256,512]{1,0:T(8,128)(2,1)} %k_hbm.1, bf16[256,512]{1,0:T(8,128)(2,1)} %v_hbm.1, bf16[4096,4096]{1,0:T(8,128)(2,1)} %w_hbm.1), custom_call_target="tpu_custom_call" | custom-call | tf_op jit(solution)/shard_map/pallas_call | solution.py:220
  71.8 2.3 %copy.6 = bf16[256,2048]{1,0:T(8,128)(2,1)} copy(bf16[256,2048]{1,0:T(8,128)(2,1)} %shard_map.46) | data formatting | bytes 2097152

commit v3 on v2

--- a/solution.py
+++ b/solution.py
@@ -15,7 +15,8 @@
 
 def kernel(dims, q_hbm, k_hbm, v_hbm, w_hbm, out_ref,
            qs, kvg, wv, acc, top, att, sendbuf, recvbuf,
-           q_sem, kv_sem, w_sem, zs_sem, ss_sem, zr_sem, sr_sem, ys_sem, yr_sem):
+           q_sem, kv_sem, w_sem, zs_sem, ss_sem, zr_sem, sr_sem, ys_sem, yr_sem,
+           relay1, relay2, r1r_sem, r1s_sem, r2r_sem, r2s_sem):
     C, N, tok, n_kv, group, n_out, width, n_chunk = dims
     c = lax.axis_index("context")
     t = lax.axis_index("tensor")
@@ -24,6 +25,11 @@
     sibling = c + 1 - 2 * odd
     has_up = c + 2 < C
     has_down = c >= 2
+    n_send = (N - 1) * n_chunk
+    half = width // 2
+    is_last = (c >= C - 2) & (C >= 6)
+    is_relay = (c < 2) & (C >= 6)
+    far = jnp.where(c < 2, c + C - 2, odd)
     factor = float(HD ** -0.5 * np.log2(np.e))
 
     def own_copy(kv, head):
@@ -57,7 +63,12 @@
 
     for d in range(1, N):
         pl.semaphore_signal(barrier, inc=1, device_id={"tensor": lax.rem(t + d, N)})
-    pl.semaphore_wait(barrier, N + has_up.astype(jnp.int32) + has_down.astype(jnp.int32))
+
+    @pl.when(is_last | is_relay)
+    def _():
+        pl.semaphore_signal(barrier, inc=1, device_id={"context": far})
+
+    pl.semaphore_wait(barrier, N + (is_last | is_relay).astype(jnp.int32) + has_up.astype(jnp.int32) + has_down.astype(jnp.int32))
 
     def up_copy(head, b):
         return pltpu.make_async_remote_copy(
@@ -162,35 +173,87 @@
             lanes = pl.ds(pl.multiple_of((head * group + g) * HD, HD), HD)
             att[:, lanes] = (a[:, :HD] / a[:, HD:]).astype(BF16)
 
-    def y_copy(i):
-        d = i // n_chunk + 1
-        return pltpu.make_async_remote_copy(
-            src_ref=sendbuf.at[i], dst_ref=recvbuf.at[i],
-            send_sem=ys_sem.at[i], recv_sem=yr_sem.at[i],
-            device_id={"tensor": lax.rem(t + d, N)})
+    def y_peer(i):
+        return {"tensor": lax.rem(t + i // n_chunk + 1, N)}
+
+    def slot(i):
+        return i // 8 * 3 + i % 8 // 2
+
+    def y_copy(i, h):
+        return pltpu.make_async_remote_copy(
+            src_ref=sendbuf.at[i, h], dst_ref=recvbuf.at[i, h],
+            send_sem=ys_sem.at[i, h], recv_sem=yr_sem.at[i, h], device_id=y_peer(i))
+
+    def down_copy(i, h):
+        return pltpu.make_async_remote_copy(
+            src_ref=sendbuf.at[i, h], dst_ref=relay1.at[slot(i), h],
+            send_sem=ys_sem.at[i, h], recv_sem=r1r_sem.at[slot(i), h], device_id={"context": far})
+
+    def cross_copy(i, h):
+        return pltpu.make_async_remote_copy(
+            src_ref=relay1.at[slot(i), h], dst_ref=relay2.at[slot(i), h],
+            send_sem=r1s_sem.at[slot(i), h], recv_sem=r2r_sem.at[slot(i), h], device_id=y_peer(i))
+
+    def back_copy(i, h):
+        return pltpu.make_async_remote_copy(
+            src_ref=relay2.at[slot(i), h], dst_ref=recvbuf.at[i, h],
+            send_sem=r2s_sem.at[slot(i), h], recv_sem=yr_sem.at[i, h], device_id={"context": far})
 
     def project(chunk):
         w_copy(chunk).wait()
         cols = pl.ds(pl.multiple_of(chunk * width, width), width)
         return jnp.dot(att[...], wv[:, cols], preferred_element_type=F32).astype(BF16)
 
-    @pl.loop(0, (N - 1) * n_chunk)
+    @pl.loop(0, n_send)
     def _(i):
         peer = lax.rem(t + i // n_chunk + 1, N)
-        sendbuf[i] = project(peer * n_chunk + i % n_chunk)
-        y_copy(i).start()
+        term = project(peer * n_chunk + i % n_chunk)
+        detour = is_last & (i % 8 < 5) & (i % 2 == 0)
+        for h in range(2):
+            sendbuf[i, h] = term[:, h * half:(h + 1) * half]
+
+        @pl.when(detour)
+        def _():
+            for h in range(2):
+                down_copy(i, h).start()
+
+        @pl.when(jnp.logical_not(detour))
+        def _():
+            for h in range(2):
+                y_copy(i, h).start()
+
+    def order(jj):
+        return jnp.where(jj < n_chunk // 2, 2 * jj + 1, 2 * (jj - n_chunk // 2))
 
     @pl.loop(0, n_chunk)
-    def _(j):
+    def _(jj):
+        j = order(jj)
         total = project(t * n_chunk + j).astype(F32)
-        for d in range(N - 1):
-            y_copy(d * n_chunk + j).wait_recv()
-            total = total + recvbuf[d * n_chunk + j].astype(F32)
-        out_ref[:, pl.ds(pl.multiple_of(j * width, width), width)] = total.astype(BF16)
-
-    @pl.loop(0, (N - 1) * n_chunk)
+        for h in range(2):
+            part = total[:, h * half:(h + 1) * half]
+            for d in range(N - 1):
+                y_copy(d * n_chunk + j, h).wait_recv()
+                part = part + recvbuf[d * n_chunk + j, h].astype(F32)
+            out_ref[:, pl.ds(pl.multiple_of(j * width + h * half, half), half)] = part.astype(BF16)
+
+    @pl.when(is_relay)
+    def _():
+        subs = [(i, h) for i in range(n_send) if i % 8 in (0, 2, 4) for h in range(2)]
+        for n in range(len(subs) + 2):
+            if n < len(subs):
+                down_copy(*subs[n]).wait_recv()
+                cross_copy(*subs[n]).start()
+            if n >= 2:
+                cross_copy(*subs[n - 2]).wait_recv()
+                back_copy(*subs[n - 2]).start()
+        for sub in subs:
+            cross_copy(*sub).wait_send()
+            back_copy(*sub).wait_send()
+
+    @pl.loop(0, n_send)
     def _(i):
-        y_copy(i).wait_send()
+        for h in range(2):
+            y_copy(i, h).wait_send()
 
     @pl.when(has_up)
     def _():
@@ -216,6 +279,7 @@
     n_chunk = own_width // width
     dims = (C, N, tok, n_kv, group, n_out, width, n_chunk)
     n_send = (N - 1) * n_chunk
+    n_det = (n_send + 7) // 8 * 3
     dma = pltpu.SemaphoreType.DMA
     return pl.pallas_call(
         functools.partial(kernel, dims),
@@ -229,8 +293,8 @@
             pltpu.VMEM((n_kv, group * tok, 2 * HD), F32),
             pltpu.VMEM((n_kv, group * tok, HD), F32),
             pltpu.VMEM((tok, q_width), BF16),
-            pltpu.VMEM((n_send, tok, width), BF16),
-            pltpu.VMEM((n_send, tok, width), BF16),
+            pltpu.VMEM((n_send, 2, tok, width // 2), BF16),
+            pltpu.VMEM((n_send, 2, tok, width // 2), BF16),
             dma((n_kv * group,)),
             dma((2, n_kv)),
             dma((N * n_chunk,)),
@@ -238,8 +302,14 @@
             dma((n_kv, C)),
             dma((n_kv, C)),
             dma((n_kv, C)),
-            dma((n_send,)),
-            dma((n_send,)),
+            dma((n_send, 2)),
+            dma((n_send, 2)),
+            pltpu.VMEM((n_det, 2, tok, width // 2), BF16),
+            pltpu.VMEM((n_det, 2, tok, width // 2), BF16),
+            dma((n_det, 2)),
+            dma((n_det, 2)),
+            dma((n_det, 2)),
+            dma((n_det, 2)),
         ],
         compiler_params=pltpu.CompilerParams(
             collective_id=0, has_side_effects=True, vmem_limit_bytes=67043328

time: 74.9 us -> 71.1 us (0.949)
  Pallas kernels: 71.8 us -> 68.1 us
    pallas_call x1, Pallas kernels: 71.8 us -> 68.1 us  [body(): pl.pallas_call(functools.partial(kernel, dims), out_shape=jax.ShapeDtypeS...]
where the time goes in v3:
time: 71.1 us; the launch traced here: 70.4 us
  Pallas kernels  68.1 us (96%)
  local copies, waits for them, and re-layouts  2.3 us (3%)
    pallas_call x1, Pallas kernels, body(): pl.pallas_call(functools.partial(kernel, dims), out_shape=jax.ShapeDtypeS...  68.1 us
    unnamed x1, local copies, waits for them, and re-layouts  2.3 us

profile of v3, /device:TPU:24, one launch (start us, length us, event | category | flops | bytes accessed | tf_op | source)
XLA Modules:
  0.0 70.4 jit_solution(955559596223515458)
XLA Ops:
  0.0 68.1 %shard_map.46 = bf16[256,2048]{1,0:T(8,128)(2,1)} custom-call(bf16[256,4096]{1,0:T(8,128)(2,1)} %q_hbm.1, bf16[256,512]{1,0:T(8,128)(2,1)} %k_hbm.1, bf16[256,512]{1,0:T(8,128)(2,1)} %v_hbm.1, bf16[4096,4096]{1,0:T(8,128)(2,1)} %w_hbm.1), custom_call_target="tpu_custom_call" | custom-call | tf_op jit(solution)/shard_map/pallas_call | solution.py:284
  68.1 2.3 %copy.6 = bf16[256,2048]{1,0:T(8,128)(2,1)} copy(bf16[256,2048]{1,0:T(8,128)(2,1)} %shard_map.46) | data formatting | bytes 2097152

commit v4 on v3

--- a/solution.py
+++ b/solution.py
@@ -222,19 +222,23 @@
             for h in range(2):
                 y_copy(i, h).start()
 
+    @pl.loop(0, n_chunk)
+    def _(j):
+        out_ref[:, pl.ds(pl.multiple_of(j * width, width), width)] = project(t * n_chunk + j)
+
     def order(jj):
         return jnp.where(jj < n_chunk // 2, 2 * jj + 1, 2 * (jj - n_chunk // 2))
 
     @pl.loop(0, n_chunk)
     def _(jj):
         j = order(jj)
-        total = project(t * n_chunk + j).astype(F32)
         for h in range(2):
-            part = total[:, h * half:(h + 1) * half]
+            cols = pl.ds(pl.multiple_of(j * width + h * half, half), half)
+            part = out_ref[:, cols].astype(F32)
             for d in range(N - 1):
                 y_copy(d * n_chunk + j, h).wait_recv()
                 part = part + recvbuf[d * n_chunk + j, h].astype(F32)
-            out_ref[:, pl.ds(pl.multiple_of(j * width + h * half, half), half)] = part.astype(BF16)
+            out_ref[:, cols] = part.astype(BF16)
 
     @pl.when(is_relay)
     def _():

time: 71.1 us -> 70.5 us (level)
  Pallas kernels: 68.1 us -> 67.3 us
    pallas_call x1, Pallas kernels: 68.1 us -> 67.3 us  [body(): pl.pallas_call(functools.partial(kernel, dims), out_shape=jax.ShapeDtypeS...]
where the time goes in v4:
time: 70.5 us; the launch traced here: 69.6 us
  Pallas kernels  67.3 us (95%)
  local copies, waits for them, and re-layouts  2.3 us (3%)
    pallas_call x1, Pallas kernels, body(): pl.pallas_call(functools.partial(kernel, dims), out_shape=jax.ShapeDtypeS...  67.3 us
    unnamed x1, local copies, waits for them, and re-layouts  2.3 us

profile of v4, /device:TPU:24, one launch (start us, length us, event | category | flops | bytes accessed | tf_op | source)
XLA Modules:
  0.0 69.6 jit_solution(14834314470372157969)
XLA Ops:
  0.0 67.3 %shard_map.46 = bf16[256,2048]{1,0:T(8,128)(2,1)} custom-call(bf16[256,4096]{1,0:T(8,128)(2,1)} %q_hbm.1, bf16[256,512]{1,0:T(8,128)(2,1)} %k_hbm.1, bf16[256,512]{1,0:T(8,128)(2,1)} %v_hbm.1, bf16[4096,4096]{1,0:T(8,128)(2,1)} %w_hbm.1), custom_call_target="tpu_custom_call" | custom-call | tf_op jit(solution)/shard_map/pallas_call | solution.py:288
  67.3 2.3 %copy.6 = bf16[256,2048]{1,0:T(8,128)(2,1)} copy(bf16[256,2048]{1,0:T(8,128)(2,1)} %shard_map.46) | data formatting | bytes 2097152

commit v5 on v4

--- a/solution.py
+++ b/solution.py
@@ -208,7 +208,7 @@
     def _(i):
         peer = lax.rem(t + i // n_chunk + 1, N)
         term = project(peer * n_chunk + i % n_chunk)
-        detour = is_last & (i % 8 < 5) & (i % 2 == 0)
+        detour = is_last & (i % 8 < 3) & (i % 2 == 0)
         for h in range(2):
             sendbuf[i, h] = term[:, h * half:(h + 1) * half]
 
@@ -242,7 +242,7 @@
 
     @pl.when(is_relay)
     def _():
-        subs = [(i, h) for i in range(n_send) if i % 8 in (0, 2, 4) for h in range(2)]
+        subs = [(i, h) for i in range(n_send) if i % 8 in (0, 2) for h in range(2)]
         for n in range(len(subs) + 2):
             if n < len(subs):
                 down_copy(*subs[n]).wait_recv()

time: 70.5 us -> 70.8 us (level)
  no operation moved by 1% of the time
where the time goes in v5:
time: 70.8 us; the launch traced here: 70 us
  Pallas kernels  67.7 us (96%)
  local copies, waits for them, and re-layouts  2.3 us (3%)
    pallas_call x1, Pallas kernels, body(): pl.pallas_call(functools.partial(kernel, dims), out_shape=jax.ShapeDtypeS...  67.7 us
    unnamed x1, local copies, waits for them, and re-layouts  2.3 us

profile of v5, /device:TPU:24, one launch (start us, length us, event | category | flops | bytes accessed | tf_op | source)
XLA Modules:
  0.0 70.0 jit_solution(7111746338605264081)
XLA Ops:
  0.0 67.7 %shard_map.46 = bf16[256,2048]{1,0:T(8,128)(2,1)} custom-call(bf16[256,4096]{1,0:T(8,128)(2,1)} %q_hbm.1, bf16[256,512]{1,0:T(8,128)(2,1)} %k_hbm.1, bf16[256,512]{1,0:T(8,128)(2,1)} %v_hbm.1, bf16[4096,4096]{1,0:T(8,128)(2,1)} %w_hbm.1), custom_call_target="tpu_custom_call" | custom-call | tf_op jit(solution)/shard_map/pallas_call | solution.py:288
  67.7 2.3 %copy.6 = bf16[256,2048]{1,0:T(8,128)(2,1)} copy(bf16[256,2048]{1,0:T(8,128)(2,1)} %shard_map.46) | data formatting | bytes 2097152
